TPU v7x, 32 devices: a whole 2x2x4 slice. The times are simulated.
32 devices in a mesh: loop: 16 (over z, x, core), ch: 2 (over y).
Axes of the slice: x: 2, y: 2, z: 4, core: 2. Of those that a mesh axis runs over, the one named last changes fastest.
Arguments:
- genome: bfloat16 [8192, 1536], P('loop', 'ch'), may hold values from -6 to 6
- dilated_kernel_weight: bfloat16 [2, 3, 1536, 768], P(None, None, 'ch', 'loop'), may hold values from -0.09375 to 0.09375
- pointwise_weight: bfloat16 [2, 768, 1536], P(None, 'loop', 'ch'), may hold values from -0.21875 to 0.21875
- bottleneck_scale: float32 [2, 768], replicated, may hold values from 0.5 to 2
- bottleneck_shift: float32 [2, 768], replicated, may hold values from -3 to 3
- output_scale: float32 [2, 1536], P(None, 'ch'), may hold values from 0.3 to 1.5
- output_shift: float32 [2, 1536], P(None, 'ch'), may hold values from -2 to 2
Outputs:
- trunk_out: bfloat16 [8192, 1536], P('loop', 'ch')
All inputs are finite; a program needn't handle non-finite values.
Results may differ from a plain program's by a relative error of at most 0.008.
Values may be sent and summed in bfloat16 or wider, within the bound.
A program may use at most 64 MiB of HBM per device.

v0:
```python
import functools

import jax
import jax.numpy as jnp
from jax import lax
from jax.experimental import pallas as pl
from jax.experimental.pallas import tpu as pltpu
from jax.sharding import PartitionSpec as P

MESH = pl.DeviceIdType.MESH
CORES = 2
TILE = 16
PIECES = 2


def gelu(v):
    return 0.5 * v * (1.0 + jnp.tanh(0.7978845608028654 * (v + 0.044715 * (v * v * v))))


def from_behind(x, axis, by):
    peers = lax.axis_size(axis)
    return lax.ppermute(x, axis, [(i, (i + by) % peers) for i in range(peers)])


def plain_shards(genome, kernel_w, point_w, mid_scale, mid_shift, out_scale, out_shift):
    state = genome
    for b in range(2):
        act = jax.nn.gelu(state.astype(jnp.float32)).astype(jnp.bfloat16)
        before = from_behind(act, "loop", b + 1)
        after = from_behind(act, "loop", -(b + 1))
        kernels = lax.all_gather(kernel_w[b], "loop", axis=2, tiled=True)
        projection = lax.all_gather(point_w[b], "loop", axis=0, tiled=True)
        mid = jnp.dot(before, kernels[0], preferred_element_type=jnp.float32)
        mid = mid + jnp.dot(act, kernels[1], preferred_element_type=jnp.float32)
        mid = mid + jnp.dot(after, kernels[2], preferred_element_type=jnp.float32)
        mid = lax.psum(mid, "ch")
        hid = jax.nn.gelu(mid * mid_scale[b] + mid_shift[b]).astype(jnp.bfloat16)
        proj = jnp.dot(hid, projection, preferred_element_type=jnp.float32)
        state = (state.astype(jnp.float32) + proj * out_scale[b] + out_shift[b]).astype(jnp.bfloat16)
    return state


def kernel(
    peers, xs, x_ref, k_ref, p_ref, m_ref, os_ref, ot_ref, o_ref,
    state, act, wbuf, mid, psend, precv, acc, res, cols,
    in_s, in_r, out_s, out_r, wr, wp, wx, wu, wd, wq, ys, yr, loc,
):
    rows, width = x_ref.shape
    part = rows // peers
    slab = p_ref.shape[1]
    zs = peers // (CORES * xs)
    chunk = slab * CORES * xs
    me = lax.axis_index("loop")
    half = lax.axis_index("ch")
    c = lax.rem(me, CORES)
    x = lax.rem(me // CORES, xs)
    z = me // (CORES * xs)
    pad = 2 * part

    def rowset(i):
        return pl.ds(pl.multiple_of(i * part, part), part)

    def a2a_in(to):
        return pltpu.make_async_remote_copy(
            src_ref=x_ref.at[rowset(to)], dst_ref=state.at[rowset(me)],
            send_sem=in_s.at[to], recv_sem=in_r.at[me],
            device_id={"loop": to}, device_id_type=MESH)

    def a2a_in_recv(i):
        frm = lax.rem(me + i, peers)
        return pltpu.make_async_remote_copy(
            src_ref=x_ref.at[rowset(frm)], dst_ref=state.at[rowset(frm)],
            send_sem=in_s.at[frm], recv_sem=in_r.at[frm],
            device_id={"loop": frm}, device_id_type=MESH)

    def a2a_out(to):
        return pltpu.make_async_remote_copy(
            src_ref=res.at[rowset(to)], dst_ref=o_ref.at[rowset(me)],
            send_sem=out_s.at[to], recv_sem=out_r.at[me],
            device_id={"loop": to}, device_id_type=MESH)

    def a2a_out_recv(i):
        frm = lax.rem(me + i, peers)
        return pltpu.make_async_remote_copy(
            src_ref=res.at[rowset(frm)], dst_ref=o_ref.at[rowset(frm)],
            send_sem=out_s.at[frm], recv_sem=out_r.at[frm],
            device_id={"loop": frm}, device_id_type=MESH)

    def plane(s):
        low = jnp.where(z < zs // 2, z, zs - 1 - z)
        at = jnp.where(s <= low, low - s, s)
        return jnp.where(z < zs // 2, at, zs - 1 - at)

    def to_all(copy, prepare=None):
        group = CORES * xs
        spot = lax.rem(me, group)

        @pl.loop(0, zs - 1)
        def _(k):
            base = lax.rem(z + 1 + k, zs) * group
            if prepare is not None:
                prepare(base, group)
            for j in range(group):
                copy(base + lax.rem(spot + j, group)).start()

        if prepare is not None:
            prepare(z * group, group)
        for j in range(1, group):
            copy(z * group + lax.rem(spot + j, group)).start()

    def index(zi, xi, ci):
        return (zi * xs + xi) * CORES + ci

    def place(b, h, owner):
        return wbuf.at[b, pl.ds(h * (4 // PIECES), 4 // PIECES), pl.ds(pl.multiple_of(owner * slab, slab), slab), :]

    def wcopy(b, h, owner, to, sem):
        return pltpu.make_async_remote_copy(
            src_ref=place(b, h, owner),
            dst_ref=place(b, h, owner),
            send_sem=sem, recv_sem=wr.at[b, h, owner],
            device_id={"loop": to}, device_id_type=MESH)

    def got(b, h, owner):
        wcopy(b, h, owner, lax.rem(me + 1, peers), wp.at[b, h, 0]).wait_recv()

    def along(b, h, s, act_on):
        zp = plane(s)
        owner = index(zp, x, c)

        @pl.when((zp <= z) & (z < zs - 1))
        def _():
            act_on(wcopy(b, h, owner, index(lax.rem(z + 1, zs), x, c), wu.at[b, h, s]))

        @pl.when((zp >= z) & (z > 0))
        def _():
            act_on(wcopy(b, h, owner, index(lax.rem(z + zs - 1, zs), x, c), wd.at[b, h, s]))

    def across(b, h, s, act_on):
        owner = index(plane(s), x, c)
        for j in range(1, xs):
            act_on(wcopy(b, h, owner, index(z, lax.rem(x + j, xs), c), wx.at[b, h, s * (xs - 1) + j - 1]))
        act_on(wcopy(b, h, owner, index(z, x, 1 - c), wp.at[b, h, s]))

    def start(copy):
        copy.start()

    def sent(copy):
        copy.wait_send()

    def forward_column(b, s):
        for h in range(PIECES):
            got(b, h, index(plane(s), x, c))
            along(b, h, s, start)
            across(b, h, s, start)

    def to_partner(b, h, s, j):
        owner = index(plane(s), lax.rem(x + j, xs), c)
        return wcopy(b, h, owner, index(z, x, 1 - c), wq.at[b, h, s * (xs - 1) + j - 1])

    def forward_across(b, s):
        for h in range(PIECES):
            for j in range(1, xs):
                got(b, h, index(plane(s), lax.rem(x + j, xs), c))
                to_partner(b, h, s, j).start()

    def arrived(b, s):
        for h in range(PIECES):
            for j in range(xs):
                got(b, h, index(plane(s), j, 1 - c))

    def ycopy(b, s):
        return pltpu.make_async_remote_copy(
            src_ref=psend.at[b, s], dst_ref=precv.at[b, s],
            send_sem=ys.at[b, s], recv_sem=yr.at[b, s],
            device_id={"ch": 1 - half}, device_id_type=MESH)

    def chunk_of(s):
        return pl.ds(pl.multiple_of(plane(s) * chunk, chunk), chunk)

    nt = (((1,), (1,)), ((), ()))
    tn = (((0,), (0,)), ((), ()))

    def middle(b, s):
        at = chunk_of(s)
        shift = (b + 1) * part
        total = None
        for t in range(3):
            term = lax.dot_general(
                wbuf[b, t, at, :], act[pl.ds(pad + (t - 1) * shift, rows), :], nt,
                preferred_element_type=jnp.float32)
            total = term if total is None else total + term
        mid[s] = total
        psend[b, s] = total.astype(jnp.bfloat16)
        ycopy(b, s).start()

    def project(b, s):
        at = chunk_of(s)
        ycopy(b, s).wait_recv()
        total = mid[s] + precv[b, s].astype(jnp.float32)
        hid = gelu(total * cols[at, pl.ds(b, 1)] + cols[at, pl.ds(2 + b, 1)]).astype(jnp.bfloat16)
        acc[...] += lax.dot_general(hid, wbuf[b, 3, at, :], tn, preferred_element_type=jnp.float32)

    step = 64 if rows % 64 == 0 else part

    def activate(src):
        @pl.loop(0, rows // step)
        def _(i):
            at = pl.ds(pl.multiple_of(i * step, step), step)
            act[pl.ds(pl.multiple_of(pad + i * step, part), step), :] = gelu(
                src[at, :].astype(jnp.float32)).astype(jnp.bfloat16)

        act[pl.ds(0, pad), :] = act[pl.ds(rows, pad), :]
        act[pl.ds(pad + rows, pad), :] = act[pl.ds(pad, pad), :]

    def update(b, src, dst):
        @pl.loop(0, rows // step)
        def _(i):
            at = pl.ds(pl.multiple_of(i * step, step), step)
            dst[at, :] = (
                src[at, :].astype(jnp.float32)
                + acc[at, :] * os_ref[pl.ds(b, 1), :] + ot_ref[pl.ds(b, 1), :]
            ).astype(jnp.bfloat16)

    def finish(first, count):
        at = pl.ds(pl.multiple_of(first * part, part), count * part)
        res[at, :] = (
            state[at, :].astype(jnp.float32) + acc[at, :] * os_ref[pl.ds(1, 1), :] + ot_ref[pl.ds(1, 1), :]
        ).astype(jnp.bfloat16)

    own_x = pltpu.make_async_copy(x_ref.at[rowset(me)], state.at[rowset(me)], loc.at[0])
    own_w = []
    for b in range(2):
        at = pl.ds(pl.multiple_of(me * slab, slab), slab)
        own_w.append(pltpu.make_async_copy(k_ref.at[b], wbuf.at[b, pl.ds(0, 3), at, :], loc.at[1 + 2 * b]))
        own_w.append(pltpu.make_async_copy(p_ref.at[b], wbuf.at[b, 3, at, :], loc.at[2 + 2 * b]))
    for copy in own_w:
        copy.start()
    own_x.start()
    cols[...] = m_ref[...].T

    barrier = pltpu.get_barrier_semaphore()

    @pl.loop(1, peers)
    def _(i):
        pl.semaphore_signal(barrier, inc=1, device_id={"loop": lax.rem(me + i, peers)}, device_id_type=MESH)

    pl.semaphore_signal(barrier, inc=1, device_id={"ch": 1 - half}, device_id_type=MESH)
    pl.semaphore_wait(barrier, peers)

    to_all(a2a_in)
    for copy in own_w:
        copy.wait()
    for h in range(PIECES):
        along(0, h, 0, start)
        across(0, h, 0, start)
    own_x.wait()

    @pl.loop(1, peers)
    def _(i):
        a2a_in_recv(i).wait_recv()

    forward_column(0, 1)
    activate(state)
    for b in range(2):
        acc[...] = jnp.zeros_like(acc)

        @pl.loop(0, zs + 1)
        def _(s):
            if b == 0:
                @pl.when((s > 0) & (s + 1 < zs))
                def _():
                    forward_column(0, s + 1)

                @pl.when(s + 2 == zs)
                def _():
                    for h in range(PIECES):
                        along(1, h, 0, start)
                        across(1, h, 0, start)

            @pl.when(s < zs)
            def _():
                forward_across(b, s)
                arrived(b, s)
                middle(b, s)

            if b == 0:
                @pl.when(s >= zs - 1)
                def _():
                    forward_column(1, s - zs + 2)
            else:
                @pl.when(s + 3 < zs)
                def _():
                    forward_column(1, s + 3)

            @pl.when(s > 0)
            def _():
                project(b, s - 1)

        if b == 0:
            update(0, state, state)
            activate(state)
        else:
            to_all(a2a_out, finish)

    own_o = pltpu.make_async_copy(res.at[rowset(me)], o_ref.at[rowset(me)], loc.at[0])
    own_o.start()
    own_o.wait()

    for b in range(2):
        for h in range(PIECES):
            along(b, h, 0, sent)
            across(b, h, 0, sent)

        @pl.loop(0, zs)
        def _(s):
            for h in range(PIECES):
                @pl.when(s > 0)
                def _():
                    along(b, h, s, sent)
                    across(b, h, s, sent)

                for j in range(1, xs):
                    to_partner(b, h, s, j).wait_send()
            ycopy(b, s).wait_send()

    @pl.loop(1, peers)
    def _(i):
        a2a_in(lax.rem(me + i, peers)).wait_send()
        a2a_out_recv(i).wait_recv()
        a2a_out(lax.rem(me + i, peers)).wait_send()


def fused_shards(genome, kernel_w, point_w, mid_scale, mid_shift, out_scale, out_shift):
    peers = lax.axis_size("loop")
    rows, width = genome.shape
    slab = point_w.shape[1]
    mids = mid_scale.shape[1]
    xs = 2
    zs = peers // (CORES * xs)
    chunk = slab * CORES * xs
    part = rows // peers
    bf16, f32 = jnp.bfloat16, jnp.float32
    dma = pltpu.SemaphoreType.DMA
    hbm = pl.BlockSpec(memory_space=pltpu.HBM)
    vmem = pl.BlockSpec(memory_space=pltpu.VMEM)
    return pl.pallas_call(
        functools.partial(kernel, peers, xs),
        out_shape=jax.ShapeDtypeStruct((rows, width), bf16),
        in_specs=[hbm] * 3 + [vmem] * 3,
        out_specs=vmem,
        scratch_shapes=[
            pltpu.VMEM((rows, width), bf16),
            pltpu.VMEM((rows + 4 * part, width), bf16),
            pltpu.VMEM((2, 4, mids, width), bf16),
            pltpu.VMEM((zs, chunk, rows), f32),
            pltpu.VMEM((2, zs, chunk, rows), bf16),
            pltpu.VMEM((2, zs, chunk, rows), bf16),
            pltpu.VMEM((rows, width), f32),
            pltpu.VMEM((rows, width), bf16),
            pltpu.VMEM((mids, 8), f32),
            dma((peers,)), dma((peers,)), dma((peers,)), dma((peers,)),
            dma((2, PIECES, peers)), dma((2, PIECES, zs)), dma((2, PIECES, zs * (xs - 1))),
            dma((2, PIECES, zs)), dma((2, PIECES, zs)), dma((2, PIECES, zs * (xs - 1))),
            dma((2, zs)), dma((2, zs)), dma((5,)),
        ],
        compiler_params=pltpu.CompilerParams(
            collective_id=0, has_side_effects=True, vmem_limit_bytes=48 * 1024 * 1024),
    )(genome, jnp.swapaxes(kernel_w, 2, 3), point_w, jnp.concatenate([mid_scale, mid_shift] * 2), out_scale, out_shift)


def shards(genome, kernel_w, *rest):
    peers = lax.axis_size("loop")
    rows, width = genome.shape
    slab = kernel_w.shape[3]
    fits = (
        peers % (CORES * 2) == 0 and rows % (peers * TILE) == 0 and slab % TILE == 0
        and width % 128 == 0 and rows % 128 == 0 and lax.axis_size("ch") == 2
    )
    return (fused_shards if fits else plain_shards)(genome, kernel_w, *rest)


def solution(mesh):
    in_specs = (
        P("loop", "ch"),
        P(None, None, "ch", "loop"),
        P(None, "loop", "ch"),
        P(),
        P(),
        P(None, "ch"),
        P(None, "ch"),
    )
    return jax.shard_map(shards, mesh=mesh, in_specs=in_specs, out_specs=P("loop", "ch"), check_vma=False)
```

profile of v0, /device:TPU:17, one launch (start us, length us, event | category | flops | bytes accessed | tf_op | source)
XLA Modules:
  0.0 104.0 jit_solution(16882528043611173808)
XLA Ops:
  0.0 0.0 copy-start.3
  0.0 0.0 copy-start.4
  0.0 0.8 pad_maximum_fusion.m_ref
  0.8 0.0 copy-done.3
  0.8 0.0 copy-done.4
  0.8 0.0 copy-start
  0.8 1.1 %copy-done = bf16[512,768]{1,0:T(8,128)(2,1)S(1)} copy-done((bf16[512,768]{1,0:T(8,128)(2,1)S(1)}, bf16[512,768]{1,0:T(8,128)(2,1)}, u32[]{:S(2)}) %copy-start) | copy-done | bytes 786456
  2.0 0.0 copy-start.1
  2.0 1.0 copy-done.1
  3.0 0.0 copy-start.2
  3.0 0.9 copy-done.2
  3.9 99.3 %shard_map.73 = bf16[512,768]{1,0:T(8,128)(2,1)S(1)} custom-call(bf16[512,768]{1,0:T(8,128)(2,1)S(1)} %copy-done, bf16[2,3,48,768]{3,2,1,0:T(8,128)(2,1)S(1)} %bitcast.1, bf16[2,48,768]{2,1,0:T(8,128)(2,1)S(1)} %copy-done.2, f32[8,768]{1,0:T(8,128)S(1)} %pad_maximum_fusion.m_ref, f32[2,768]{1,0:T(2,128)S(1)} %copy-done.3, f32[2,768]{1,0:T(2,128)S(1)} %copy-done.4), custom_call_target="tpu_custom_call" | custom-call | tf_op jit(solution)/shard_map/pallas_call | solution.py:347
  103.2 0.9 copy.9
Async XLA Ops:
  0.0 0.8 copy-start.3
  0.0 0.8 copy-start.4
  0.8 1.1 %copy-start = (bf16[512,768]{1,0:T(8,128)(2,1)S(1)}, bf16[512,768]{1,0:T(8,128)(2,1)}, u32[]{:S(2)}) copy-start(bf16[512,768]{1,0:T(8,128)(2,1)} %x_ref.1) | copy-start | bytes 2359300
  2.0 1.0 copy-start.1
  3.0 0.9 copy-start.2
where the time goes:
time: 105 us; the launch traced here: 104 us
  Pallas kernels  99.3 us (95%)
  local copies, waits for them, and re-layouts  3.94 us (4%)
    pallas_call x1, Pallas kernels, fused_shards(): pl.pallas_call(functools.partial(kernel, peers, xs), out_shape=jax.ShapeD...  99.3 us
    unnamed x11, local copies, waits for them, and re-layouts  3.94 us

commit v1 on v0

--- a/solution.py
+++ b/solution.py
@@ -11,6 +11,10 @@
 CORES = 2
 TILE = 16
 PIECES = 2
+VMEM_BYTES = 67043328
+TO_OUTER = ((1, 0),)
+TO_INNER = ((0, 1), (1, 0), (1, 1))
+HALVES = 2
 
 
 def gelu(v):
@@ -41,9 +45,9 @@
 
 
 def kernel(
-    peers, xs, x_ref, k_ref, p_ref, m_ref, os_ref, ot_ref, o_ref,
-    state, act, wbuf, mid, psend, precv, acc, res, cols,
-    in_s, in_r, out_s, out_r, wr, wp, wx, wu, wd, wq, ys, yr, loc,
+    peers, xs, x_ref, k_ref, p_ref, ms_ref, mt_ref, os_ref, ot_ref, o_ref,
+    state, act, wbuf, mid, psend, precv, acc, res, cols, coef, lmid, lsend, lrecv,
+    in_s, in_r, out_s, out_r, wr, wp, wx, wu, wd, wq, we, ys, yr, yls, ylr, loc,
 ):
     rows, width = x_ref.shape
     part = rows // peers
@@ -136,11 +140,45 @@
         def _():
             act_on(wcopy(b, h, owner, index(lax.rem(z + zs - 1, zs), x, c), wd.at[b, h, s]))
 
+    edge = jnp.where(z % 2 == 0, z + 1, z - 1)
+    outer = (z == 0) | (z == zs - 1)
+
+    def by_edge(b, h, corner):
+        return (b, h) in (TO_INNER if corner else TO_OUTER)
+
+    def over_x(b, h, s):
+        may = not isinstance(s, int) or s == 1
+        skip_outer = may and by_edge(b, h, False)
+        skip_inner = may and by_edge(b, h, True)
+        keep = z >= 0
+        if skip_outer:
+            keep = keep & jnp.logical_not(outer & (s == 1))
+        if skip_inner:
+            keep = keep & (outer | (s != 1))
+        return keep
+
     def across(b, h, s, act_on):
         owner = index(plane(s), x, c)
-        for j in range(1, xs):
-            act_on(wcopy(b, h, owner, index(z, lax.rem(x + j, xs), c), wx.at[b, h, s * (xs - 1) + j - 1]))
+
+        @pl.when(over_x(b, h, s))
+        def _():
+            for j in range(1, xs):
+                act_on(wcopy(b, h, owner, index(z, lax.rem(x + j, xs), c), wx.at[b, h, s * (xs - 1) + j - 1]))
+
         act_on(wcopy(b, h, owner, index(z, x, 1 - c), wp.at[b, h, s]))
+
+    def past_edge(b, h, act_on):
+        if not by_edge(b, h, True) and not by_edge(b, h, False):
+            return
+        copy = wcopy(b, h, index(z, 1 - x, c), index(edge, x, c), we.at[b, h])
+        if by_edge(b, h, True):
+            @pl.when(outer)
+            def _():
+                act_on(copy)
+        if by_edge(b, h, False):
+            @pl.when(jnp.logical_not(outer))
+            def _():
+                act_on(copy)
 
     def start(copy):
         copy.start()
@@ -162,6 +200,11 @@
         for h in range(PIECES):
             for j in range(1, xs):
                 got(b, h, index(plane(s), lax.rem(x + j, xs), c))
+
+                @pl.when(s == 0)
+                def _():
+                    past_edge(b, h, start)
+
                 to_partner(b, h, s, j).start()
 
     def arrived(b, s):
@@ -234,83 +277,176 @@
         at = pl.ds(pl.multiple_of(me * slab, slab), slab)
         own_w.append(pltpu.make_async_copy(k_ref.at[b], wbuf.at[b, pl.ds(0, 3), at, :], loc.at[1 + 2 * b]))
         own_w.append(pltpu.make_async_copy(p_ref.at[b], wbuf.at[b, 3, at, :], loc.at[2 + 2 * b]))
+
+    barrier = pltpu.get_barrier_semaphore()
+
+    @pl.loop(1, peers)
+    def _(i):
+        pl.semaphore_signal(barrier, inc=1, device_id={"loop": lax.rem(me + i, peers)}, device_id_type=MESH)
+
+    pl.semaphore_signal(barrier, inc=1, device_id={"ch": 1 - half}, device_id_type=MESH)
     for copy in own_w:
         copy.start()
     own_x.start()
-    cols[...] = m_ref[...].T
-
-    barrier = pltpu.get_barrier_semaphore()
-
-    @pl.loop(1, peers)
-    def _(i):
-        pl.semaphore_signal(barrier, inc=1, device_id={"loop": lax.rem(me + i, peers)}, device_id_type=MESH)
-
-    pl.semaphore_signal(barrier, inc=1, device_id={"ch": 1 - half}, device_id_type=MESH)
-    pl.semaphore_wait(barrier, peers)
-
-    to_all(a2a_in)
+    coef[...] = jnp.zeros_like(coef)
+    coef[pl.ds(0, 2), :] = ms_ref[...]
+    coef[pl.ds(2, 2), :] = mt_ref[...]
+    cols[...] = coef[...].T
+    acc[...] = jnp.zeros_like(acc)
     for copy in own_w:
         copy.wait()
-    for h in range(PIECES):
-        along(0, h, 0, start)
-        across(0, h, 0, start)
     own_x.wait()
+    pl.semaphore_wait(barrier, peers)
+
+    def own_slab(b):
+        for h in range(PIECES):
+            along(b, h, 0, start)
+            across(b, h, 0, start)
+
+    inner = jnp.logical_not(outer)
+
+    own_slab(0)
+    to_all(a2a_in)
+    forward_column(0, 1)
+
+    @pl.when(outer)
+    def _():
+        own_slab(1)
+
+    @pl.when(inner)
+    def _():
+        forward_column(0, 2)
+        own_slab(1)
 
     @pl.loop(1, peers)
     def _(i):
         a2a_in_recv(i).wait_recv()
 
-    forward_column(0, 1)
     activate(state)
-    for b in range(2):
-        acc[...] = jnp.zeros_like(acc)
-
-        @pl.loop(0, zs + 1)
-        def _(s):
-            if b == 0:
-                @pl.when((s > 0) & (s + 1 < zs))
+
+    @pl.loop(0, zs + 1)
+    def _(s):
+        @pl.when(s < zs)
+        def _():
+            forward_across(0, s)
+            arrived(0, s)
+            middle(0, s)
+
+        @pl.when(outer & (s == 0))
+        def _():
+            forward_column(0, 2)
+
+        @pl.when((outer & (s == 2)) | (inner & (s == 1)))
+        def _():
+            forward_column(0, 3)
+
+        @pl.when((outer & (s == 3)) | (inner & (s == 2)))
+        def _():
+            forward_column(1, 1)
+
+        @pl.when(inner & (s == 3))
+        def _():
+            forward_column(1, 2)
+
+        @pl.when(s > 0)
+        def _():
+            project(0, s - 1)
+
+    update(0, state, state)
+    activate(state)
+    acc[...] = jnp.zeros_like(acc)
+
+    @pl.loop(0, zs - 1)
+    def _(s):
+        forward_across(1, s)
+        arrived(1, s)
+        middle(1, s)
+
+        @pl.when(outer & (s == 0))
+        def _():
+            forward_column(1, 2)
+
+        @pl.when((outer & (s == 1)) | (inner & (s == 0)))
+        def _():
+            forward_column(1, 3)
+
+        @pl.when(s > 0)
+        def _():
+            project(1, s - 1)
+
+    project(1, zs - 2)
+    last = zs - 1
+    forward_across(1, last)
+    arrived(1, last)
+    group = CORES * xs
+    level = group * part
+    far = jnp.where(z < zs // 2, 1, 0)
+    span = rows // HALVES
+    last_at = chunk_of(last)
+    shift = 2 * part
+
+    def halfset(q):
+        return pl.ds(pl.multiple_of(q * span, span), span)
+
+    def lcopy(k):
+        return pltpu.make_async_remote_copy(
+            src_ref=lsend.at[k], dst_ref=lrecv.at[k],
+            send_sem=yls.at[k], recv_sem=ylr.at[k],
+            device_id={"ch": 1 - half}, device_id_type=MESH)
+
+    def to_half(k):
+        return jnp.where(far == 1, 1 - k, k) if HALVES == 2 else k
+
+    for k in range(HALVES):
+        q = to_half(k)
+        total = None
+        for t in range(3):
+            term = lax.dot_general(
+                wbuf[1, t, last_at, :],
+                act[pl.ds(pl.multiple_of(pad + (t - 1) * shift + q * span, part), span), :], nt,
+                preferred_element_type=jnp.float32)
+            total = term if total is None else total + term
+        lmid[k] = total
+        lsend[k] = total.astype(jnp.bfloat16)
+        lcopy(k).start()
+
+    for k in range(HALVES):
+        q = to_half(k)
+        lcopy(k).wait_recv()
+        total = lmid[k] + lrecv[k].astype(jnp.float32)
+        hid = gelu(total * cols[last_at, pl.ds(1, 1)] + cols[last_at, pl.ds(3, 1)]).astype(jnp.bfloat16)
+        acc[halfset(q), :] += lax.dot_general(hid, wbuf[1, 3, last_at, :], tn, preferred_element_type=jnp.float32)
+
+        def send_level(zt):
+            finish(zt * group, group)
+            spot = lax.rem(me, group)
+            for j in range(group):
+                to = zt * group + lax.rem(spot + j, group)
+
+                @pl.when(to != me)
                 def _():
-                    forward_column(0, s + 1)
-
-                @pl.when(s + 2 == zs)
-                def _():
-                    for h in range(PIECES):
-                        along(1, h, 0, start)
-                        across(1, h, 0, start)
-
-            @pl.when(s < zs)
-            def _():
-                forward_across(b, s)
-                arrived(b, s)
-                middle(b, s)
-
-            if b == 0:
-                @pl.when(s >= zs - 1)
-                def _():
-                    forward_column(1, s - zs + 2)
-            else:
-                @pl.when(s + 3 < zs)
-                def _():
-                    forward_column(1, s + 3)
-
-            @pl.when(s > 0)
-            def _():
-                project(b, s - 1)
-
-        if b == 0:
-            update(0, state, state)
-            activate(state)
-        else:
-            to_all(a2a_out, finish)
+                    a2a_out(to).start()
+
+        per = zs // HALVES
+
+        @pl.loop(0, per)
+        def _(i):
+            at = jnp.where(z < zs // 2, per - 1 - i, i)
+            send_level(q * per + at)
 
     own_o = pltpu.make_async_copy(res.at[rowset(me)], o_ref.at[rowset(me)], loc.at[0])
     own_o.start()
     own_o.wait()
+
+    @pl.loop(1, peers)
+    def _(i):
+        a2a_out_recv(i).wait_recv()
 
     for b in range(2):
         for h in range(PIECES):
             along(b, h, 0, sent)
             across(b, h, 0, sent)
+            past_edge(b, h, sent)
 
         @pl.loop(0, zs)
         def _(s):
@@ -322,12 +458,17 @@
 
                 for j in range(1, xs):
                     to_partner(b, h, s, j).wait_send()
-            ycopy(b, s).wait_send()
+
+            @pl.when((s < zs - 1) | (b == 0))
+            def _():
+                ycopy(b, s).wait_send()
+
+    for k in range(HALVES):
+        lcopy(k).wait_send()
 
     @pl.loop(1, peers)
     def _(i):
         a2a_in(lax.rem(me + i, peers)).wait_send()
-        a2a_out_recv(i).wait_recv()
         a2a_out(lax.rem(me + i, peers)).wait_send()
 
 
@@ -347,7 +488,7 @@
     return pl.pallas_call(
         functools.partial(kernel, peers, xs),
         out_shape=jax.ShapeDtypeStruct((rows, width), bf16),
-        in_specs=[hbm] * 3 + [vmem] * 3,
+        in_specs=[hbm] * 3 + [vmem] * 4,
         out_specs=vmem,
         scratch_shapes=[
             pltpu.VMEM((rows, width), bf16),
@@ -359,14 +500,18 @@
             pltpu.VMEM((rows, width), f32),
             pltpu.VMEM((rows, width), bf16),
             pltpu.VMEM((mids, 8), f32),
+            pltpu.VMEM((8, mids), f32),
+            pltpu.VMEM((HALVES, chunk, rows // HALVES), f32),
+            pltpu.VMEM((HALVES, chunk, rows // HALVES), bf16),
+            pltpu.VMEM((HALVES, chunk, rows // HALVES), bf16),
             dma((peers,)), dma((peers,)), dma((peers,)), dma((peers,)),
             dma((2, PIECES, peers)), dma((2, PIECES, zs)), dma((2, PIECES, zs * (xs - 1))),
             dma((2, PIECES, zs)), dma((2, PIECES, zs)), dma((2, PIECES, zs * (xs - 1))),
-            dma((2, zs)), dma((2, zs)), dma((5,)),
+            dma((2, PIECES)), dma((2, zs)), dma((2, zs)), dma((HALVES,)), dma((HALVES,)), dma((5,)),
         ],
         compiler_params=pltpu.CompilerParams(
-            collective_id=0, has_side_effects=True, vmem_limit_bytes=48 * 1024 * 1024),
-    )(genome, jnp.swapaxes(kernel_w, 2, 3), point_w, jnp.concatenate([mid_scale, mid_shift] * 2), out_scale, out_shift)
+            collective_id=0, has_side_effects=True, vmem_limit_bytes=VMEM_BYTES),
+    )(genome, jnp.swapaxes(kernel_w, 2, 3), point_w, mid_scale, mid_shift, out_scale, out_shift)
 
 
 def shards(genome, kernel_w, *rest):
@@ -374,7 +519,7 @@
     rows, width = genome.shape
     slab = kernel_w.shape[3]
     fits = (
-        peers % (CORES * 2) == 0 and rows % (peers * TILE) == 0 and slab % TILE == 0
+        peers == CORES * 2 * 4 and rows % (peers * TILE) == 0 and slab % TILE == 0
         and width % 128 == 0 and rows % 128 == 0 and lax.axis_size("ch") == 2
     )
     return (fused_shards if fits else plain_shards)(genome, kernel_w, *rest)

time: 105 us -> 112 us (1.067)
  Pallas kernels: 99.3 us -> 109 us
  local copies, waits for them, and re-layouts: 3.94 us -> 2.06 us
    pallas_call x1, Pallas kernels: 99.3 us -> 109 us  [fused_shards(): pl.pallas_call(functools.partial(kernel, peers, xs), out_shape=jax.ShapeD...]
    unnamed x11 -> x1, local copies, waits for them, and re-layouts: 3.94 us -> 2.06 us
where the time goes in v1:
time: 112 us
  Pallas kernels  109 us (97%)
  local copies, waits for them, and re-layouts  2.06 us (2%)
    pallas_call x1, Pallas kernels, fused_shards(): pl.pallas_call(functools.partial(kernel, peers, xs), out_shape=jax.ShapeD...  109 us

profile of v1, /device:TPU:17, one launch (start us, length us, event | category | flops | bytes accessed | tf_op | source)
XLA Modules:
  0.0 111.5 jit_solution(11888705161420812061)
XLA Ops:
  0.0 109.4 %shard_map.73 = bf16[512,768]{1,0:T(8,128)(2,1)} custom-call(bf16[512,768]{1,0:T(8,128)(2,1)} %x_ref.1, bf16[2,3,48,768]{3,2,1,0:T(8,128)(2,1)} %bitcast.1, bf16[2,48,768]{2,1,0:T(8,128)(2,1)} %p_ref.1, f32[2,768]{1,0:T(2,128)} %ms_ref.1, f32[2,768]{1,0:T(2,128)} %mt_ref.1, f32[2,768]{1,0:T(2,128)} %os_ref.1, f32[2,768]{1,0:T(2,128)} %ot_ref.1), custom_call_target="tpu_custom_call" | custom-call | tf_op jit(solution)/shard_map/pallas_call | solution.py:488
  109.4 2.1 %copy.9 = bf16[512,768]{1,0:T(8,128)(2,1)} copy(bf16[512,768]{1,0:T(8,128)(2,1)} %shard_map.73) | data formatting | bytes 1572864

commit v2 on v1

--- a/solution.py
+++ b/solution.py
@@ -11,9 +11,9 @@
 CORES = 2
 TILE = 16
 PIECES = 2
-VMEM_BYTES = 67043328
-TO_OUTER = ((1, 0),)
-TO_INNER = ((0, 1), (1, 0), (1, 1))
+VMEM_BYTES = 50331648
+TO_OUTER = ()
+TO_INNER = ((1, 0), (1, 1))
 HALVES = 2
 
 
@@ -45,8 +45,8 @@
 
 
 def kernel(
-    peers, xs, x_ref, k_ref, p_ref, ms_ref, mt_ref, os_ref, ot_ref, o_ref,
-    state, act, wbuf, mid, psend, precv, acc, res, cols, coef, lmid, lsend, lrecv,
+    peers, xs, x_ref, k_ref, p_ref, ms_ref, mt_ref, osh_ref, oth_ref, o_ref,
+    state, act, wbuf, mid, psend, precv, acc, res, cols, coef, os_ref, ot_ref, lmid, lsend, lrecv,
     in_s, in_r, out_s, out_r, wr, wp, wx, wu, wd, wq, we, ys, yr, yls, ylr, loc,
 ):
     rows, width = x_ref.shape
@@ -289,13 +289,21 @@
         copy.start()
     own_x.start()
     coef[...] = jnp.zeros_like(coef)
-    coef[pl.ds(0, 2), :] = ms_ref[...]
-    coef[pl.ds(2, 2), :] = mt_ref[...]
-    cols[...] = coef[...].T
+    small = [
+        pltpu.make_async_copy(ms_ref, coef.at[pl.ds(0, 2)], loc.at[5]),
+        pltpu.make_async_copy(mt_ref, coef.at[pl.ds(2, 2)], loc.at[6]),
+        pltpu.make_async_copy(osh_ref, os_ref, loc.at[7]),
+        pltpu.make_async_copy(oth_ref, ot_ref, loc.at[8]),
+    ]
+    for copy in small:
+        copy.start()
     acc[...] = jnp.zeros_like(acc)
     for copy in own_w:
         copy.wait()
     own_x.wait()
+    for copy in small:
+        copy.wait()
+    cols[...] = coef[...].T
     pl.semaphore_wait(barrier, peers)
 
     def own_slab(b):
@@ -309,19 +317,21 @@
     to_all(a2a_in)
     forward_column(0, 1)
 
-    @pl.when(outer)
-    def _():
-        own_slab(1)
-
     @pl.when(inner)
     def _():
         forward_column(0, 2)
-        own_slab(1)
 
     @pl.loop(1, peers)
     def _(i):
         a2a_in_recv(i).wait_recv()
 
+    for h in range(PIECES):
+        across(1, h, 0, start)
+
+        @pl.when(outer)
+        def _():
+            along(1, h, 0, start)
+
     activate(state)
 
     @pl.loop(0, zs + 1)
@@ -336,17 +346,30 @@
         def _():
             forward_column(0, 2)
 
+        @pl.when(inner & (s == 0))
+        def _():
+            along(1, 0, 0, start)
+
+        @pl.when((outer & (s == 1)) | (inner & (s == 0)))
+        def _():
+            forward_column(0, 3)
+
+        @pl.when(inner & (s == 0))
+        def _():
+            along(1, 1, 0, start)
+
         @pl.when((outer & (s == 2)) | (inner & (s == 1)))
         def _():
-            forward_column(0, 3)
+            forward_across(1, 0)
+            forward_column(1, 1)
 
         @pl.when((outer & (s == 3)) | (inner & (s == 2)))
         def _():
-            forward_column(1, 1)
+            forward_column(1, 2)
 
         @pl.when(inner & (s == 3))
         def _():
-            forward_column(1, 2)
+            forward_column(1, 3)
 
         @pl.when(s > 0)
         def _():
@@ -356,26 +379,25 @@
     activate(state)
     acc[...] = jnp.zeros_like(acc)
 
-    @pl.loop(0, zs - 1)
+    last = zs - 1
+
+    @pl.loop(0, last)
     def _(s):
-        forward_across(1, s)
+        @pl.when(s > 0)
+        def _():
+            forward_across(1, s)
+
         arrived(1, s)
         middle(1, s)
 
-        @pl.when(outer & (s == 0))
-        def _():
-            forward_column(1, 2)
-
-        @pl.when((outer & (s == 1)) | (inner & (s == 0)))
+        @pl.when(outer & (s == 1))
         def _():
             forward_column(1, 3)
 
-        @pl.when(s > 0)
-        def _():
-            project(1, s - 1)
-
-    project(1, zs - 2)
-    last = zs - 1
+    @pl.loop(0, last - 1)
+    def _(s):
+        project(1, s)
+
     forward_across(1, last)
     arrived(1, last)
     group = CORES * xs
@@ -409,6 +431,8 @@
         lmid[k] = total
         lsend[k] = total.astype(jnp.bfloat16)
         lcopy(k).start()
+
+    project(1, last - 1)
 
     for k in range(HALVES):
         q = to_half(k)
@@ -485,10 +509,11 @@
     dma = pltpu.SemaphoreType.DMA
     hbm = pl.BlockSpec(memory_space=pltpu.HBM)
     vmem = pl.BlockSpec(memory_space=pltpu.VMEM)
+    operands = (genome, jnp.swapaxes(kernel_w, 2, 3), point_w, mid_scale, mid_shift, out_scale, out_shift)
     return pl.pallas_call(
         functools.partial(kernel, peers, xs),
         out_shape=jax.ShapeDtypeStruct((rows, width), bf16),
-        in_specs=[hbm] * 3 + [vmem] * 4,
+        in_specs=[hbm] * len(operands),
         out_specs=vmem,
         scratch_shapes=[
             pltpu.VMEM((rows, width), bf16),
@@ -501,17 +526,19 @@
             pltpu.VMEM((rows, width), bf16),
             pltpu.VMEM((mids, 8), f32),
             pltpu.VMEM((8, mids), f32),
+            pltpu.VMEM((2, width), f32),
+            pltpu.VMEM((2, width), f32),
             pltpu.VMEM((HALVES, chunk, rows // HALVES), f32),
             pltpu.VMEM((HALVES, chunk, rows // HALVES), bf16),
             pltpu.VMEM((HALVES, chunk, rows // HALVES), bf16),
             dma((peers,)), dma((peers,)), dma((peers,)), dma((peers,)),
             dma((2, PIECES, peers)), dma((2, PIECES, zs)), dma((2, PIECES, zs * (xs - 1))),
             dma((2, PIECES, zs)), dma((2, PIECES, zs)), dma((2, PIECES, zs * (xs - 1))),
-            dma((2, PIECES)), dma((2, zs)), dma((2, zs)), dma((HALVES,)), dma((HALVES,)), dma((5,)),
+            dma((2, PIECES)), dma((2, zs)), dma((2, zs)), dma((HALVES,)), dma((HALVES,)), dma((9,)),
         ],
         compiler_params=pltpu.CompilerParams(
             collective_id=0, has_side_effects=True, vmem_limit_bytes=VMEM_BYTES),
-    )(genome, jnp.swapaxes(kernel_w, 2, 3), point_w, mid_scale, mid_shift, out_scale, out_shift)
+    )(*(pltpu.with_memory_space_constraint(a, pltpu.HBM) for a in operands))
 
 
 def shards(genome, kernel_w, *rest):

time: 112 us -> 97.3 us (0.87)
  Pallas kernels: 109 us -> 96.3 us
  local copies, waits for them, and re-layouts: 2.06 us -> 0.88 us
    pallas_call x1, Pallas kernels: 109 us -> 96.3 us  [fused_shards(): pl.pallas_call(functools.partial(kernel, peers, xs), out_shape=jax.ShapeD...]
    unnamed x1, local copies, waits for them, and re-layouts: 2.06 us -> 0.88 us
where the time goes in v2:
time: 97.3 us; the launch traced here: 97.2 us
  Pallas kernels  96.3 us (99%)
    pallas_call x1, Pallas kernels, fused_shards(): pl.pallas_call(functools.partial(kernel, peers, xs), out_shape=jax.ShapeD...  96.3 us

profile of v2, /device:TPU:17, one launch (start us, length us, event | category | flops | bytes accessed | tf_op | source)
XLA Modules:
  0.0 97.2 jit_solution(11521812608222569682)
XLA Ops:
  0.0 96.3 %shard_map.73 = bf16[512,768]{1,0:T(8,128)(2,1)S(1)} custom-call(bf16[512,768]{1,0:T(8,128)(2,1)} %x_ref.1, bf16[2,3,48,768]{3,2,1,0:T(8,128)(2,1)} %bitcast.1, bf16[2,48,768]{2,1,0:T(8,128)(2,1)} %p_ref.1, f32[2,768]{1,0:T(2,128)} %ms_ref.1, f32[2,768]{1,0:T(2,128)} %mt_ref.1, f32[2,768]{1,0:T(2,128)} %osh_ref.1, f32[2,768]{1,0:T(2,128)} %oth_ref.1), custom_call_target="tpu_custom_call" | custom-call | tf_op jit(solution)/shard_map/pallas_call | solution.py:513
  96.3 0.9 copy.9

commit v3 on v2

--- a/solution.py
+++ b/solution.py
@@ -13,7 +13,7 @@
 PIECES = 2
 VMEM_BYTES = 50331648
 TO_OUTER = ()
-TO_INNER = ((1, 0), (1, 1))
+TO_INNER = ((0, 0), (0, 1), (1, 0), (1, 1))
 HALVES = 2
 
 
@@ -315,30 +315,35 @@
 
     own_slab(0)
     to_all(a2a_in)
+    for h in range(PIECES):
+        across(1, h, 0, start)
+
+        @pl.when(outer)
+        def _():
+            along(1, h, 0, start)
+
     forward_column(0, 1)
 
     @pl.when(inner)
     def _():
         forward_column(0, 2)
 
+    forward_across(0, 0)
+
     @pl.loop(1, peers)
     def _(i):
         a2a_in_recv(i).wait_recv()
 
-    for h in range(PIECES):
-        across(1, h, 0, start)
-
-        @pl.when(outer)
-        def _():
-            along(1, h, 0, start)
-
     activate(state)
 
     @pl.loop(0, zs + 1)
     def _(s):
         @pl.when(s < zs)
         def _():
-            forward_across(0, s)
+            @pl.when(s > 0)
+            def _():
+                forward_across(0, s)
+
             arrived(0, s)
             middle(0, s)
 
@@ -363,7 +368,7 @@
             forward_across(1, 0)
             forward_column(1, 1)
 
-        @pl.when((outer & (s == 3)) | (inner & (s == 2)))
+        @pl.when(inner & (s == 2))
         def _():
             forward_column(1, 2)
 
@@ -374,6 +379,10 @@
         @pl.when(s > 0)
         def _():
             project(0, s - 1)
+
+        @pl.when(outer & (s == 3))
+        def _():
+            forward_column(1, 2)
 
     update(0, state, state)
     activate(state)
@@ -394,9 +403,7 @@
         def _():
             forward_column(1, 3)
 
-    @pl.loop(0, last - 1)
-    def _(s):
-        project(1, s)
+    project(1, 0)
 
     forward_across(1, last)
     arrived(1, last)
@@ -430,9 +437,12 @@
             total = term if total is None else total + term
         lmid[k] = total
         lsend[k] = total.astype(jnp.bfloat16)
-        lcopy(k).start()
-
+        if k == 0:
+            lcopy(k).start()
+
+    project(1, last - 2)
     project(1, last - 1)
+    lcopy(1).start()
 
     for k in range(HALVES):
         q = to_half(k)

time: 97.3 us -> 95.1 us (0.977)
  Pallas kernels: 96.3 us -> 94.1 us
    pallas_call x1, Pallas kernels: 96.3 us -> 94.1 us  [fused_shards(): pl.pallas_call(functools.partial(kernel, peers, xs), out_shape=jax.ShapeD...]
where the time goes in v3:
time: 95.1 us; the launch traced here: 95 us
  Pallas kernels  94.1 us (99%)
    pallas_call x1, Pallas kernels, fused_shards(): pl.pallas_call(functools.partial(kernel, peers, xs), out_shape=jax.ShapeD...  94.1 us

profile of v3, /device:TPU:17, one launch (start us, length us, event | category | flops | bytes accessed | tf_op | source)
XLA Modules:
  0.0 95.0 jit_solution(10908622162604659294)
XLA Ops:
  0.0 94.1 %shard_map.73 = bf16[512,768]{1,0:T(8,128)(2,1)S(1)} custom-call(bf16[512,768]{1,0:T(8,128)(2,1)} %x_ref.1, bf16[2,3,48,768]{3,2,1,0:T(8,128)(2,1)} %bitcast.1, bf16[2,48,768]{2,1,0:T(8,128)(2,1)} %p_ref.1, f32[2,768]{1,0:T(2,128)} %ms_ref.1, f32[2,768]{1,0:T(2,128)} %mt_ref.1, f32[2,768]{1,0:T(2,128)} %osh_ref.1, f32[2,768]{1,0:T(2,128)} %oth_ref.1), custom_call_target="tpu_custom_call" | custom-call | tf_op jit(solution)/shard_map/pallas_call | solution.py:523
  94.1 0.9 copy.9

commit v4 on v3

--- a/solution.py
+++ b/solution.py
@@ -237,12 +237,16 @@
         psend[b, s] = total.astype(jnp.bfloat16)
         ycopy(b, s).start()
 
-    def project(b, s):
+    def project(b, s, first=False):
         at = chunk_of(s)
         ycopy(b, s).wait_recv()
         total = mid[s] + precv[b, s].astype(jnp.float32)
         hid = gelu(total * cols[at, pl.ds(b, 1)] + cols[at, pl.ds(2 + b, 1)]).astype(jnp.bfloat16)
-        acc[...] += lax.dot_general(hid, wbuf[b, 3, at, :], tn, preferred_element_type=jnp.float32)
+        term = lax.dot_general(hid, wbuf[b, 3, at, :], tn, preferred_element_type=jnp.float32)
+        if first:
+            acc[...] = term
+        else:
+            acc[...] += term
 
     step = 64 if rows % 64 == 0 else part
 
@@ -253,17 +257,25 @@
             act[pl.ds(pl.multiple_of(pad + i * step, part), step), :] = gelu(
                 src[at, :].astype(jnp.float32)).astype(jnp.bfloat16)
 
+        wrap()
+
+    def wrap():
         act[pl.ds(0, pad), :] = act[pl.ds(rows, pad), :]
         act[pl.ds(pad + rows, pad), :] = act[pl.ds(pad, pad), :]
 
-    def update(b, src, dst):
+    def advance():
         @pl.loop(0, rows // step)
         def _(i):
             at = pl.ds(pl.multiple_of(i * step, step), step)
-            dst[at, :] = (
-                src[at, :].astype(jnp.float32)
-                + acc[at, :] * os_ref[pl.ds(b, 1), :] + ot_ref[pl.ds(b, 1), :]
+            new = (
+                state[at, :].astype(jnp.float32)
+                + acc[at, :] * os_ref[pl.ds(0, 1), :] + ot_ref[pl.ds(0, 1), :]
             ).astype(jnp.bfloat16)
+            state[at, :] = new
+            act[pl.ds(pl.multiple_of(pad + i * step, part), step), :] = gelu(
+                new.astype(jnp.float32)).astype(jnp.bfloat16)
+
+        wrap()
 
     def finish(first, count):
         at = pl.ds(pl.multiple_of(first * part, part), count * part)
@@ -384,9 +396,7 @@
         def _():
             forward_column(1, 2)
 
-    update(0, state, state)
-    activate(state)
-    acc[...] = jnp.zeros_like(acc)
+    advance()
 
     last = zs - 1
 
@@ -403,7 +413,7 @@
         def _():
             forward_column(1, 3)
 
-    project(1, 0)
+    project(1, 0, first=True)
 
     forward_across(1, last)
     arrived(1, last)

time: 95.1 us -> 95 us (level)
  no operation moved by 1% of the time
where the time goes in v4:
time: 95 us; the launch traced here: 94.8 us
  Pallas kernels  93.9 us (99%)
    pallas_call x1, Pallas kernels, fused_shards(): pl.pallas_call(functools.partial(kernel, peers, xs), out_shape=jax.ShapeD...  93.9 us

profile of v4, /device:TPU:17, one launch (start us, length us, event | category | flops | bytes accessed | tf_op | source)
XLA Modules:
  0.0 94.8 jit_solution(3202811381421503682)
XLA Ops:
  0.0 93.9 %shard_map.73 = bf16[512,768]{1,0:T(8,128)(2,1)S(1)} custom-call(bf16[512,768]{1,0:T(8,128)(2,1)} %x_ref.1, bf16[2,3,48,768]{3,2,1,0:T(8,128)(2,1)} %bitcast.1, bf16[2,48,768]{2,1,0:T(8,128)(2,1)} %p_ref.1, f32[2,768]{1,0:T(2,128)} %ms_ref.1, f32[2,768]{1,0:T(2,128)} %mt_ref.1, f32[2,768]{1,0:T(2,128)} %osh_ref.1, f32[2,768]{1,0:T(2,128)} %oth_ref.1), custom_call_target="tpu_custom_call" | custom-call | tf_op jit(solution)/shard_map/pallas_call | solution.py:533
  93.9 0.9 copy.9
